TPU v7x, 32 devices: a whole 2x2x4 slice. The times are simulated.
32 devices in a mesh: replica: 8 (over z, core), shard: 4 (over y, x).
Axes of the slice: x: 2, y: 2, z: 4, core: 2. Of those that a mesh axis runs over, the one named last changes fastest.
Arguments:
- local_weights: bfloat16 [8, 8192, 512], P('replica', 'shard'), may hold values from -1.3258252 to 1.3258252
- outer_base: bfloat16 [8192, 512], P('shard'), may hold values from -0.0625 to 0.0625
- momentum: bfloat16 [8192, 512], P('shard', 'replica'), may hold values from -0.06591797 to 0.06591797
- error_feedback: bfloat16 [8, 8192, 512], P('replica', 'shard'), may hold values from -0.032958984 to 0.032958984
- q_start: float32 [512, 32], replicated, may hold values from -6 to 6
- tokens: bfloat16 [8, 512, 8192], P('replica', None, 'shard'), may hold values from -6 to 6
Outputs:
- new_base: bfloat16 [8192, 512], P('shard')
- new_momentum: bfloat16 [8192, 512], P('shard', 'replica')
- new_error: bfloat16 [8, 8192, 512], P('replica', 'shard')
- key_rows: bfloat16 [8, 512, 512], P('replica', 'shard')
All inputs are finite; a program needn't handle non-finite values.
Results may differ from a plain program's by a relative error of at most 0.0065.
Values may be sent and summed in bfloat16 or wider, within the bound.
A program may use at most 64 MiB of HBM per device.

v0:
```python
import jax
import jax.numpy as jnp
from jax import lax
from jax.sharding import PartitionSpec as P

outer_mu = 0.9
outer_rate = 0.7


def on_device(local_weights, outer_base, momentum, error_feedback, q_start, tokens):
    highest = lax.Precision.HIGHEST
    replicas = lax.axis_size("replica")
    own_columns = momentum.shape[1]
    full_momentum = lax.all_gather(momentum, "replica", axis=1, tiled=True)
    pseudo = (
        outer_base.astype(jnp.float32)
        - local_weights[0].astype(jnp.float32)
        + error_feedback[0].astype(jnp.float32)
    )
    p_local = jnp.dot(pseudo, q_start, precision=highest)
    p_mean = lax.psum(p_local, "replica") / replicas
    own_gram = jnp.dot(p_mean.T, p_mean, precision=highest)
    gram_sum = lax.psum(own_gram, "shard")
    factor_low = jnp.linalg.cholesky(gram_sum)
    basis = jax.scipy.linalg.solve_triangular(factor_low, p_mean.T, lower=True).T
    q_raw = jnp.dot(pseudo.T, basis, precision=highest)
    q_mean = lax.psum(q_raw, ("replica", "shard")) / replicas
    update = jnp.dot(basis, q_mean.T, precision=highest)
    new_error = (pseudo - update).astype(jnp.bfloat16)[None]
    moment = outer_mu * full_momentum.astype(jnp.float32) + update
    new_base = (outer_base.astype(jnp.float32) - outer_rate * (outer_mu * moment + update)).astype(
        jnp.bfloat16
    )
    first_column = lax.axis_index("replica") * own_columns
    new_momentum = lax.dynamic_slice_in_dim(moment, first_column, own_columns, 1).astype(
        jnp.bfloat16
    )
    own_tokens = tokens[0]
    key_sum = lax.psum_scatter(
        jnp.dot(own_tokens, new_base, preferred_element_type=jnp.float32),
        "shard",
        scatter_dimension=0,
        tiled=True,
    )
    key_rows = key_sum.astype(jnp.bfloat16)[None]
    return (new_base, new_momentum, new_error, key_rows)


def solution(mesh):
    in_specs = (
        P("replica", "shard", None),
        P("shard", None),
        P("shard", "replica"),
        P("replica", "shard", None),
        P(),
        P("replica", None, "shard"),
    )
    out_specs = (
        P("shard", None),
        P("shard", "replica"),
        P("replica", "shard", None),
        P("replica", "shard", None),
    )
    return jax.shard_map(
        on_device, mesh=mesh, in_specs=in_specs, out_specs=out_specs, check_vma=False
    )
```

profile of v0, /device:TPU:0, one launch (start us, length us, event | category | flops | bytes accessed | tf_op | source)
XLA Modules:
  0.0 319.2 jit_solution(3947755793024692435)
XLA Ops:
  7.2 0.0 copy-start
  7.2 0.0 all-reduce.3.cloned.1.call-start
  7.2 4.1 %copy.10 = bf16[2048,512]{0,1:T(8,128)(2,1)} copy(bf16[2048,512]{1,0:T(8,128)(2,1)} %param.7) | data formatting | bytes 4194304 | tf_op args[1]
  11.3 4.0 %copy.11 = bf16[1,2048,512]{1,2,0:T(8,128)(2,1)} copy(bf16[1,2048,512]{2,1,0:T(8,128)(2,1)} %param.6) | data formatting | bytes 4194304 | tf_op args[0]
  15.3 0.0 copy-start.6
  15.3 3.9 %copy.12 = bf16[1,2048,512]{1,2,0:T(8,128)(2,1)} copy(bf16[1,2048,512]{2,1,0:T(8,128)(2,1)} %param.9) | data formatting | bytes 4194304 | tf_op args[3]
  19.2 0.0 copy-done.6
  19.2 6.8 %fusion.10 = f32[2048,32]{0,1:T(8,128)} fusion(f32[512,32]{0,1:T(8,128)S(1)} %copy-done.6, bf16[2048,512]{0,1:T(8,128)(2,1)} %copy.10, bf16[1,2048,512]{1,2,0:T(8,128)(2,1)} %copy.12, bf16[1,2048,512]{1,2,0:T(8,128)(2,1)} %copy.11), kind=kOutput, calls=%fused_computation.11 | convolution fusion | flops 407896064 | bytes 6619136 | tf_op jit(solution)/shard_map/dot_general | solution.py:20
  26.0 0.0 all-reduce.3.cloned.1.call-update
  26.0 0.0 all-reduce.5.cloned.1.call-start
  26.1 58.3 %all-reduce.3.cloned.1.call-done = f32[2048,32]{0,1:T(8,128)} async-done(((f32[2048,32]{0,1:T(8,128)}), f32[2048,32]{0,1:T(8,128)}) %all-reduce.3.cloned.1.call-update) | async-done | bytes 262160 | tf_op jit(solution)/shard_map/psum | solution.py:21
  84.3 1.4 fusion.16
  85.7 16.0 %psum.22 = f32[32,32]{0,1:T(8,128)S(1)} all-reduce(f32[32,32]{0,1:T(8,128)S(1)} %fusion.16), channel_id=1, replica_groups=mesh['replica'=8,'shard'=4] {'shard'}, use_global_device_ids=true, to_apply=%region_1.0 | all-reduce | flops 1024 | bytes 8192 | tf_op jit(solution)/shard_map/psum | solution.py:23
  101.7 0.1 copy.14
  101.8 2.9 cholesky.16
  104.7 0.6 compare_reduce_fusion
  105.4 0.7 fusion.21
  106.0 2.4 custom-call.7
  108.4 1.4 fusion.14
  109.8 6.4 %fusion.8 = f32[512,32]{1,0:T(8,128)} fusion(f32[32,2048]{1,0:T(8,128)S(1)} %fusion.14, bf16[2048,512]{0,1:T(8,128)(2,1)} %copy.10, bf16[1,2048,512]{1,2,0:T(8,128)(2,1)} %copy.12, bf16[1,2048,512]{1,2,0:T(8,128)(2,1)} %copy.11), kind=kOutput, calls=%fused_computation.10 | convolution fusion | flops 407896064 | bytes 6619136 | tf_op jit(solution)/shard_map/dot_general | solution.py:26
  116.2 0.0 all-reduce.5.cloned.1.call-update
  116.3 0.0 all-gather.2.cloned.1.call-start
  116.3 0.7 all-gather.2.cloned.1.call-update
  117.0 0.2 reduce-scatter.2.cloned.1.call-start
  117.2 123.0 %all-reduce.5.cloned.1.call-done = f32[512,32]{1,0:T(8,128)} async-done(((f32[512,32]{1,0:T(8,128)}), f32[512,32]{1,0:T(8,128)}) %all-reduce.5.cloned.1.call-update) | async-done | bytes 65552 | tf_op jit(solution)/shard_map/psum | solution.py:27
  240.2 29.8 %all-gather.2.cloned.1.call-done = bf16[2048,512]{0,1:T(8,128)(2,1)} async-done(((bf16[2048,64]{0,1:T(8,128)(2,1)}), bf16[2048,512]{0,1:T(8,128)(2,1)}) %all-gather.2.cloned.1.call-update) | async-done | bytes 2097168 | tf_op jit(solution)/shard_map/all_gather | solution.py:14
  270.1 0.0 copy-start.1
  270.1 0.0 copy-start.2
  270.1 0.0 copy-start.3
  270.1 0.0 copy-start.4
  270.1 6.3 %multiply_add_fusion = (bf16[2048,512]{0,1:T(8,128)(2,1)}, f32[2048,512]{0,1:T(8,128)S(1)}) fusion(bf16[2048,512]{0,1:T(8,128)(2,1)} %all-gather.2.cloned.1.call-done, f32[32,2048]{1,0:T(8,128)S(1)} %fusion.14, f32[512,32]{1,0:T(8,128)} %all-reduce.5.cloned.1.call-done), kind=kOutput, calls=%fused_computation.5 | convolution fusion | flops 406863872 | bytes 8716288 | tf_op jit(solution)/shard_map/dot_general | solution.py:28
  276.4 0.0 copy-done.1
  276.4 0.0 copy-done.2
  276.4 0.0 copy-done.3
  276.4 0.0 copy-done.4
  276.4 3.5 %fusion.2 = (bf16[1,2048,512]{1,2,0:T(8,128)(2,1)}, bf16[2048,512]{0,1:T(8,128)(2,1)S(1)}) fusion(f32[2048,512]{0,1:T(8,128)S(1)} %get-tuple-element.11, bf16[1,2048,512]{1,2,0:T(8,128)(2,1)S(1)} %copy-done.3, bf16[1,2048,512]{1,2,0:T(8,128)(2,1)S(1)} %copy-done.2, bf16[2048,512]{0,1:T(8,128)(2,1)S(1)} %copy-done.1, bf16[2048,512]{0,1:T(8,128)(2,1)S(1)} %copy-done.4), kind=kLoop, calls=%fused_computation.6 | loop fusion | flops 15728640 | bytes 16777216 | tf_op jit(solution)/shard_map/broadcast_in_dim | solution.py:29
  279.8 0.0 copy-start.5
  279.9 1.3 copy-done.5
  281.2 0.0 copy-done
  281.2 2.3 fusion.5
  283.4 0.0 reduce-scatter.2.cloned.1.call-update
  283.5 3.9 %copy.15 = bf16[2048,512]{1,0:T(8,128)(2,1)} copy(bf16[2048,512]{0,1:T(8,128)(2,1)} %copy-done.5) | data formatting | bytes 4194304
  287.4 4.0 %copy.16 = bf16[1,2048,512]{2,1,0:T(8,128)(2,1)} copy(bf16[1,2048,512]{1,2,0:T(8,128)(2,1)} %get-tuple-element.8) | data formatting | bytes 4194304
  291.3 1.7 dynamic-slice_convert_fusion
  293.0 17.9 %reduce-scatter.2.cloned.1.call-done = f32[128,512]{0,1:T(8,128)} async-done(((f32[512,512]{0,1:T(8,128)}), f32[128,512]{0,1:T(8,128)}) %reduce-scatter.2.cloned.1.call-update) | async-done | bytes 262160 | tf_op jit(solution)/shard_map/reduce_scatter | solution.py:39
  310.9 1.0 convert_bitcast_fusion
  311.9 0.8 copy.17
  (2 shorter events, 0.0 us)
Async XLA Ops:
  7.2 274.0 %copy-start = (bf16[1,512,2048]{2,1,0:T(8,128)(2,1)S(1)}, bf16[1,512,2048]{2,1,0:T(8,128)(2,1)}, u32[]{:S(2)}) copy-start(bf16[1,512,2048]{2,1,0:T(8,128)(2,1)} %param.11) | copy-start | bytes 6291460
  7.2 77.1 %all-reduce.3.cloned.1.call-start = ((), (), s32[]{:S(2)}) async-start(), calls=%async_computation.2 | async-start | bytes 524288 | tf_op jit(solution)/shard_map/psum | solution.py:21
  15.3 3.9 %copy-start.6 = (f32[512,32]{0,1:T(8,128)S(1)}, f32[512,32]{0,1:T(8,128)}, u32[]{:S(2)}) copy-start(f32[512,32]{0,1:T(8,128)} %param.10) | copy-start | bytes 196612
  26.0 214.2 %all-reduce.5.cloned.1.call-start = ((), (), s32[]{:S(2)}) async-start(), calls=%async_computation.3 | async-start | bytes 524288 | tf_op jit(solution)/shard_map/psum | solution.py:27
  116.3 153.8 %all-gather.2.cloned.1.call-start = ((), (), s32[]{:S(2)}) async-start(), calls=%async_computation.1 | async-start | bytes 2359296 | tf_op jit(solution)/shard_map/all_gather | solution.py:14
  117.0 193.9 %reduce-scatter.2.cloned.1.call-start = ((), (), s32[]{:S(2)}) async-start(), calls=%async_computation.4 | async-start | bytes 1310720 | tf_op jit(solution)/shard_map/reduce_scatter | solution.py:39
  270.1 6.3 %copy-start.1 = (bf16[2048,512]{0,1:T(8,128)(2,1)S(1)}, bf16[2048,512]{0,1:T(8,128)(2,1)}, u32[]{:S(2)}) copy-start(bf16[2048,512]{0,1:T(8,128)(2,1)} %copy.10) | copy-start | bytes 6291460
  270.1 6.3 %copy-start.2 = (bf16[1,2048,512]{1,2,0:T(8,128)(2,1)S(1)}, bf16[1,2048,512]{1,2,0:T(8,128)(2,1)}, u32[]{:S(2)}) copy-start(bf16[1,2048,512]{1,2,0:T(8,128)(2,1)} %copy.11) | copy-start | bytes 6291460
  270.1 6.3 %copy-start.3 = (bf16[1,2048,512]{1,2,0:T(8,128)(2,1)S(1)}, bf16[1,2048,512]{1,2,0:T(8,128)(2,1)}, u32[]{:S(2)}) copy-start(bf16[1,2048,512]{1,2,0:T(8,128)(2,1)} %copy.12) | copy-start | bytes 6291460
  270.1 6.3 %copy-start.4 = (bf16[2048,512]{0,1:T(8,128)(2,1)S(1)}, bf16[2048,512]{0,1:T(8,128)(2,1)}, u32[]{:S(2)}) copy-start(bf16[2048,512]{0,1:T(8,128)(2,1)} %all-gather.2.cloned.1.call-done) | copy-start | bytes 6291460
  279.8 1.3 copy-start.5
Sparse Core Ops, SparseCore 0:
  26.1 58.1 all-reduce.2
  116.4 123.7 all-reduce.4
  241.8 28.1 all-gather.1
  283.6 27.3 reduce-scatter.1
where the time goes:
time: 320 us; the launch traced here: 319 us
  waiting for transfers between devices  230 us (72%)
  matrix products  24.5 us (8%)
  local copies, waits for them, and re-layouts  23.7 us (7%)
  blocking collectives  16 us (5%)
  between operations  13.8 us (4%)
  other arithmetic  11.1 us (3%)
    psum x1, waiting for transfers between devices, on_device(): q_mean = lax.psum(q_raw, ('replica', 'shard')) / replicas  123 us
    psum x1, waiting for transfers between devices, on_device(): p_mean = lax.psum(p_local, 'replica') / replicas  58.3 us
    all_gather x1, waiting for transfers between devices, on_device(): full_momentum = lax.all_gather(momentum, 'replica', axis=1, tiled=True)  29.8 us
    unnamed x20, local copies, waits for them, and re-layouts  22 us
    reduce_scatter x1, waiting for transfers between devices, on_device(): lax.psum_scatter(jnp.dot(own_tokens, new_base, preferred_element_type=jnp...  17.9 us
    psum x1, blocking collectives, on_device(): gram_sum = lax.psum(own_gram, 'shard')  16 us
    dot_general x1, matrix products, on_device(): p_local = jnp.dot(pseudo, q_start, precision=highest)  6.77 us
  transfers between devices with their start and end apart: 4, of which 4 were waited for; matrix products, arithmetic and copies ran while one was open for 3% of the time, Pallas kernels for 0%

commit v1 on v0

--- a/solution.py
+++ b/solution.py
@@ -11,7 +11,7 @@
     highest = lax.Precision.HIGHEST
     replicas = lax.axis_size("replica")
     own_columns = momentum.shape[1]
-    full_momentum = lax.all_gather(momentum, "replica", axis=1, tiled=True)
+    full_momentum = jnp.concatenate(lax.all_gather(momentum, "replica"), axis=1)
     pseudo = (
         outer_base.astype(jnp.float32)
         - local_weights[0].astype(jnp.float32)

time: 320 us -> 296 us (0.925)
  waiting for transfers between devices: 230 us -> 201 us
  matrix products: 24.5 us -> 28 us
    all_gather x1, waiting for transfers between devices: 29.8 us -> 0.02 us  [on_device(): full_momentum = jnp.concatenate(lax.all_gather(momentum, 'replica'), axis=1)]
    dot_general x1, matrix products: 6.28 us -> 9.8 us  [on_device(): update = jnp.dot(basis, q_mean.T, precision=highest)]
    broadcast_in_dim x1 -> x0, other arithmetic: 3.47 us -> none  [on_device(): new_error = (pseudo - update).astype(jnp.bfloat16)[None]]
    unnamed x20 -> x12, local copies, waits for them, and re-layouts: 22 us -> 21.9 us
  transfers between devices with their start and end apart: 4 -> 4, of which waited for: 4 -> 3; matrix products, arithmetic and copies ran while one was open for 3% -> 10% of each run, Pallas kernels for 0% -> 0%
where the time goes in v1:
time: 296 us; the launch traced here: 295 us
  waiting for transfers between devices  201 us (68%)
  matrix products  28 us (9%)
  local copies, waits for them, and re-layouts  25.8 us (9%)
  blocking collectives  16 us (5%)
  between operations  13.8 us (5%)
  other arithmetic  9.59 us (3%)
    psum x1, waiting for transfers between devices, on_device(): q_mean = lax.psum(q_raw, ('replica', 'shard')) / replicas  126 us
    psum x1, waiting for transfers between devices, on_device(): p_mean = lax.psum(p_local, 'replica') / replicas  57.5 us
    unnamed x12, local copies, waits for them, and re-layouts  21.9 us
    reduce_scatter x1, waiting for transfers between devices, on_device(): lax.psum_scatter(jnp.dot(own_tokens, new_base, preferred_element_type=jnp...  17.6 us
    psum x1, blocking collectives, on_device(): gram_sum = lax.psum(own_gram, 'shard')  16 us
    dot_general x1, matrix products, on_device(): update = jnp.dot(basis, q_mean.T, precision=highest)  9.8 us
    dot_general x1, matrix products, on_device(): p_local = jnp.dot(pseudo, q_start, precision=highest)  6.77 us
    dot_general x1, matrix products, on_device(): q_raw = jnp.dot(pseudo.T, basis, precision=highest)  6.43 us
  transfers between devices with their start and end apart: 4, of which 3 were waited for; matrix products, arithmetic and copies ran while one was open for 10% of the time, Pallas kernels for 0%

profile of v1, /device:TPU:0, one launch (start us, length us, event | category | flops | bytes accessed | tf_op | source)
XLA Modules:
  0.0 295.1 jit_solution(2912820521338833623)
XLA Ops:
  7.2 0.0 copy-start
  7.2 0.0 all-reduce.3.cloned.1.call-start
  7.2 4.1 %copy.10 = bf16[2048,512]{0,1:T(8,128)(2,1)} copy(bf16[2048,512]{1,0:T(8,128)(2,1)} %param.7) | data formatting | bytes 4194304 | tf_op args[1]
  11.3 3.9 %copy.13 = bf16[1,2048,512]{1,2,0:T(8,128)(2,1)} copy(bf16[1,2048,512]{2,1,0:T(8,128)(2,1)} %param.9) | data formatting | bytes 4194304 | tf_op args[3]
  15.2 0.0 copy-start.2
  15.2 4.0 %copy.12 = bf16[1,2048,512]{1,2,0:T(8,128)(2,1)} copy(bf16[1,2048,512]{2,1,0:T(8,128)(2,1)} %param.6) | data formatting | bytes 4194304 | tf_op args[0]
  19.2 0.0 copy-done.2
  19.2 6.8 %fusion.10 = f32[2048,32]{0,1:T(8,128)} fusion(f32[512,32]{0,1:T(8,128)S(1)} %copy-done.2, bf16[2048,512]{0,1:T(8,128)(2,1)} %copy.10, bf16[1,2048,512]{1,2,0:T(8,128)(2,1)} %copy.13, bf16[1,2048,512]{1,2,0:T(8,128)(2,1)} %copy.12), kind=kOutput, calls=%fused_computation.13 | convolution fusion | flops 407896064 | bytes 6619136 | tf_op jit(solution)/shard_map/dot_general | solution.py:20
  25.9 0.0 all-reduce.3.cloned.1.call-update
  26.0 0.0 all-gather.3.cloned.1.call-start
  26.0 0.7 all-gather.3.cloned.1.call-update
  26.7 0.0 all-reduce.5.cloned.1.call-start
  26.8 57.5 %all-reduce.3.cloned.1.call-done = f32[2048,32]{0,1:T(8,128)} async-done(((f32[2048,32]{0,1:T(8,128)}), f32[2048,32]{0,1:T(8,128)}) %all-reduce.3.cloned.1.call-update) | async-done | bytes 262160 | tf_op jit(solution)/shard_map/psum | solution.py:21
  84.3 1.4 fusion.16
  85.7 16.0 %psum.22 = f32[32,32]{0,1:T(8,128)S(1)} all-reduce(f32[32,32]{0,1:T(8,128)S(1)} %fusion.16), channel_id=1, replica_groups=mesh['replica'=8,'shard'=4] {'shard'}, use_global_device_ids=true, to_apply=%region_1.0 | all-reduce | flops 1024 | bytes 8192 | tf_op jit(solution)/shard_map/psum | solution.py:23
  101.6 0.1 copy.15
  101.7 2.9 cholesky.16
  104.7 0.6 compare_reduce_fusion
  105.3 0.7 fusion.21
  106.0 2.4 custom-call.7
  108.4 1.4 fusion.14
  109.8 6.4 %fusion.8 = f32[512,32]{1,0:T(8,128)} fusion(f32[32,2048]{1,0:T(8,128)S(1)} %fusion.14, bf16[2048,512]{0,1:T(8,128)(2,1)} %copy.10, bf16[1,2048,512]{1,2,0:T(8,128)(2,1)} %copy.13, bf16[1,2048,512]{1,2,0:T(8,128)(2,1)} %copy.12), kind=kOutput, calls=%fused_computation.12 | convolution fusion | flops 407896064 | bytes 6619136 | tf_op jit(solution)/shard_map/dot_general | solution.py:26
  116.2 0.0 all-reduce.5.cloned.1.call-update
  116.3 0.2 reduce-scatter.2.cloned.1.call-start
  116.5 0.0 all-gather.3.cloned.1.call-done
  116.5 1.9 convert_multiply_fusion
  118.5 2.2 copy.22
  120.7 125.6 %all-reduce.5.cloned.1.call-done = f32[512,32]{1,0:T(8,128)} async-done(((f32[512,32]{1,0:T(8,128)}), f32[512,32]{1,0:T(8,128)}) %all-reduce.5.cloned.1.call-update) | async-done | bytes 65552 | tf_op jit(solution)/shard_map/psum | solution.py:27
  246.2 9.8 %fusion.1 = (bf16[2048,512]{0,1:T(8,128)(2,1)S(1)}, bf16[2048,512]{0,1:T(8,128)(2,1)}, bf16[1,2048,512]{1,2,0:T(8,128)(2,1)}) fusion(bf16[2048,512]{0,1:T(8,128)(2,1)} %copy.10, f32[8,2048,64]{1,2,0:T(8,128)} %bitcast.48, bf16[1,2048,512]{1,2,0:T(8,128)(2,1)} %copy.13, bf16[1,2048,512]{1,2,0:T(8,128)(2,1)} %copy.12, f32[32,2048]{1,0:T(8,128)S(1)} %fusion.14, ...), kind=kOutput, calls=%fused_computation.3 | convolution fusion | flops 417349632 | bytes 17104896 | tf_op jit(solution)/shard_map/dot_general | solution.py:28
  256.0 0.0 copy-start.1
  256.0 1.3 copy-done.1
  257.4 0.0 copy-done
  257.4 2.3 fusion.5
  259.6 0.0 reduce-scatter.2.cloned.1.call-update
  259.7 3.9 %copy.16 = bf16[2048,512]{1,0:T(8,128)(2,1)} copy(bf16[2048,512]{0,1:T(8,128)(2,1)} %copy-done.1) | data formatting | bytes 4194304
  263.6 3.9 %copy.17 = bf16[1,2048,512]{2,1,0:T(8,128)(2,1)} copy(bf16[1,2048,512]{1,2,0:T(8,128)(2,1)} %get-tuple-element.10) | data formatting | bytes 4194304
  267.5 1.7 dynamic-slice_convert_fusion
  269.2 17.6 %reduce-scatter.2.cloned.1.call-done = f32[128,512]{0,1:T(8,128)} async-done(((f32[512,512]{0,1:T(8,128)}), f32[128,512]{0,1:T(8,128)}) %reduce-scatter.2.cloned.1.call-update) | async-done | bytes 262160 | tf_op jit(solution)/shard_map/reduce_scatter | solution.py:39
  286.8 1.0 convert_bitcast_fusion
  287.8 0.8 copy.18
  (2 shorter events, 0.0 us)
Async XLA Ops:
  7.2 250.2 %copy-start = (bf16[1,512,2048]{2,1,0:T(8,128)(2,1)S(1)}, bf16[1,512,2048]{2,1,0:T(8,128)(2,1)}, u32[]{:S(2)}) copy-start(bf16[1,512,2048]{2,1,0:T(8,128)(2,1)} %param.11) | copy-start | bytes 6291460
  7.2 77.1 %all-reduce.3.cloned.1.call-start = ((), (), s32[]{:S(2)}) async-start(), calls=%async_computation.1 | async-start | bytes 524288 | tf_op jit(solution)/shard_map/psum | solution.py:21
  15.2 4.0 %copy-start.2 = (f32[512,32]{0,1:T(8,128)S(1)}, f32[512,32]{0,1:T(8,128)}, u32[]{:S(2)}) copy-start(f32[512,32]{0,1:T(8,128)} %param.10) | copy-start | bytes 196612
  26.0 90.6 %all-gather.3.cloned.1.call-start = ((), (), s32[]{:S(2)}) async-start(), calls=%async_computation.4 | async-start | bytes 2359296 | tf_op jit(solution)/shard_map/all_gather | solution.py:14
  26.7 219.5 %all-reduce.5.cloned.1.call-start = ((), (), s32[]{:S(2)}) async-start(), calls=%async_computation.2 | async-start | bytes 524288 | tf_op jit(solution)/shard_map/psum | solution.py:27
  116.3 170.5 %reduce-scatter.2.cloned.1.call-start = ((), (), s32[]{:S(2)}) async-start(), calls=%async_computation.3 | async-start | bytes 1310720 | tf_op jit(solution)/shard_map/reduce_scatter | solution.py:39
  256.0 1.3 copy-start.1
Sparse Core Ops, SparseCore 0:
  26.1 58.1 all-reduce.2
  85.9 28.1 all-gather.2
  120.2 126.0 all-reduce.4
  259.8 26.9 reduce-scatter.1
